TPU v7x, 512 devices: a whole 4x8x8 slice. The times are simulated.
512 devices in a mesh: dp: 16 (over z, core), ctx: 8 (over x, y_lo), mp: 4 (over y_hi).
Axes of the slice: x: 4, y: 8 (y_hi: 4, y_lo: 2; y = y_hi * 2 + y_lo), z: 8, core: 2. Of those that a mesh axis runs over, the one named last changes fastest.
Arguments:
- queries: bfloat16 [16, 1024, 4096], P('dp', 'ctx', 'mp'), may hold values from -1.6953125 to 1.6953125
- keys: bfloat16 [16, 1024, 4096], P('dp', 'ctx', 'mp'), may hold values from -1.6953125 to 1.6953125
- values: bfloat16 [16, 1024, 4096], P('dp', 'ctx', 'mp'), may hold values from -6 to 6
- cross_queries: bfloat16 [16, 1024, 4096], P('dp', 'ctx', 'mp'), may hold values from -1.6953125 to 1.6953125
- encoded_bank: bfloat16 [16, 64, 64, 896], P('dp', 'ctx'), may hold values from -6 to 6
- key_weight: bfloat16 [896, 4096], P(('dp', 'ctx'), 'mp'), may hold values from -0.1875 to 0.1875
- value_weight: bfloat16 [896, 4096], P(('dp', 'ctx'), 'mp'), may hold values from -0.1875 to 0.1875
- owner_ids: int32 [16, 16, 2], P('dp', 'ctx'), may hold values from 0 to 15, as said below
- unit_ids: int32 [16, 16, 2], P('dp', 'ctx'), may hold values from 0 to 6
- lengths: int32 [16], P('dp'), may hold values from 64 to 1024
Outputs:
- self_core: bfloat16 [16, 1024, 4096], P('dp', 'ctx', 'mp')
- cross_core: bfloat16 [16, 1024, 4096], P('dp', 'ctx', 'mp')
Inputs may be any that keep to these rules, and one draw needn't show every extreme that they name: `owner_ids`: among the 4 neighbours of the spans of one device (aligned blocks of 2 spans), no owner is named more than once.
All inputs are finite; a program needn't handle non-finite values.
Results may differ from a plain program's by a relative error of at most 0.006.
Values may be sent and summed in bfloat16 or wider, within the bound.
No kernel may reach another device: no remote copies, remote signals or barrier semaphores. Data moves between devices by JAX's collectives and lax.ppermute only.
A program may use at most 64 MiB of HBM per device.

v0:
```python
import math
import jax
import jax.numpy as jnp
from jax import lax
from jax.sharding import PartitionSpec as P

HD = 128
SPAN = 64
NBR = 2


def attend_block(totals, query_heads, positions, key_piece, value_piece, start):
    key_count = key_piece.shape[0]
    head_count = query_heads.shape[1]
    key_heads = key_piece.reshape(key_count, head_count, HD)
    value_heads = value_piece.reshape(key_count, head_count, HD)
    block_size = 512
    last_position = positions[-1]
    for offset in range(0, key_count, block_size):
        key_block = key_heads[offset : offset + block_size]
        value_block = value_heads[offset : offset + block_size]
        block_start = start + offset

        def compute(current):
            running_sums, running_totals = current
            scores = jnp.einsum(
                "qhd,khd->hqk", query_heads, key_block, preferred_element_type=jnp.float32
            ) * (1.0 / math.sqrt(HD))
            key_pos = block_start + jnp.arange(block_size, dtype=jnp.int32)
            allowed = key_pos[None, :] <= positions[:, None]
            weights = jnp.where(allowed[None], jnp.exp(scores), 0.0)
            running_sums = running_sums + jnp.einsum(
                "hqk,khd->qhd",
                weights.astype(jnp.bfloat16),
                value_block,
                preferred_element_type=jnp.float32,
            )
            running_totals = running_totals + jnp.transpose(jnp.sum(weights, axis=2))
            return (running_sums, running_totals)

        def keep(current):
            return current

        active = jnp.logical_and(True, block_start <= last_position)
        totals = lax.cond(active, compute, keep, totals)
    return totals


def empty_totals(row_count, head_count):
    return (
        jnp.zeros((row_count, head_count, HD), jnp.float32),
        jnp.zeros((row_count, head_count), jnp.float32),
    )


def local(
    queries,
    keys,
    values,
    cross_queries,
    encoded_bank,
    key_weight,
    value_weight,
    owner_ids,
    unit_ids,
    lengths,
):
    tok_rows = queries.shape[1]
    feature_width = queries.shape[2]
    head_count = feature_width // HD
    span_count = tok_rows // SPAN
    ctx_index = lax.axis_index("ctx")
    dossier_length = lengths[0]
    positions = ctx_index * tok_rows + jnp.arange(tok_rows, dtype=jnp.int32)
    live_rows = positions < dossier_length
    query_heads = queries[0].reshape(tok_rows, head_count, HD)
    totals = attend_block(
        empty_totals(tok_rows, head_count),
        query_heads,
        positions,
        lax.all_gather(keys, "ctx", axis=1, tiled=True)[0],
        lax.all_gather(values, "ctx", axis=1, tiled=True)[0],
        jnp.int32(0),
    )
    self_heads = totals[0] / totals[1][:, :, None]
    self_core = (
        jnp.where(live_rows[:, None, None], self_heads, 0.0)
        .astype(jnp.bfloat16)
        .reshape(1, tok_rows, feature_width)
    )
    dp_count = lax.axis_size("dp")
    request_total = span_count * NBR
    capacity = -(-request_total // dp_count)
    owners_flat = owner_ids[0].reshape(request_total)
    units_flat = unit_ids[0].reshape(request_total)
    request_order = jnp.arange(request_total, dtype=jnp.int32)
    span_starts = positions[::SPAN]
    live_request = jnp.repeat(span_starts < dossier_length, NBR)
    same_owner = (owners_flat[None, :] == owners_flat[:, None]) & (
        request_order[None, :] < request_order[:, None]
    )
    rank_index = jnp.sum(same_owner.astype(jnp.int32), axis=1)
    slot_index = owners_flat * capacity + rank_index
    slot_numbers = jnp.arange(dp_count * capacity, dtype=jnp.int32)
    matches = (slot_index[:, None] == slot_numbers[None, :]) & live_request[:, None]
    requests = (jnp.sum(jnp.where(matches, units_flat[:, None] + 1, 0), axis=0) - 1).reshape(
        dp_count, capacity
    )
    enc_width = encoded_bank.shape[3]
    bank_local = encoded_bank[0]
    unit_total = bank_local.shape[0]
    asked_units = lax.all_to_all(requests, "dp", split_axis=0, concat_axis=0, tiled=True)
    present = asked_units >= 0
    leading = jnp.clip(asked_units, 0, unit_total - 2)
    joined = jnp.concatenate(
        (jnp.take(bank_local, leading, axis=0), jnp.take(bank_local, leading + 1, axis=0)), axis=2
    )
    joined = jnp.where(present[:, :, None, None], joined, jnp.zeros_like(joined))
    received = lax.all_to_all(joined, "dp", split_axis=0, concat_axis=0, tiled=True)
    own_rows = jnp.take(
        received.reshape(dp_count * capacity, 2 * SPAN, enc_width), slot_index, axis=0
    )
    full_key_weight, full_value_weight = (
        lax.all_gather(key_weight, ("dp", "ctx"), axis=0, tiled=True),
        lax.all_gather(value_weight, ("dp", "ctx"), axis=0, tiled=True),
    )
    retrieved = own_rows.reshape(request_total * 2 * SPAN, enc_width)
    key_proj = jnp.dot(retrieved, full_key_weight, preferred_element_type=jnp.float32).reshape(
        span_count, NBR * 2 * SPAN, head_count, HD
    )
    key_scale = lax.rsqrt(jnp.mean(key_proj * key_proj, axis=3, keepdims=True) + 1e-06)
    cross_keys = (key_proj * key_scale).astype(jnp.bfloat16)
    cross_values = (
        jnp.dot(retrieved, full_value_weight, preferred_element_type=jnp.float32)
        .astype(jnp.bfloat16)
        .reshape(span_count, NBR * 2 * SPAN, head_count, HD)
    )
    span_queries = cross_queries[0].reshape(span_count, SPAN, head_count, HD)
    cross_scores = jnp.einsum(
        "cqhd,ckhd->chqk", span_queries, cross_keys, preferred_element_type=jnp.float32
    ) * (1.0 / math.sqrt(HD))
    cross_weights = jnp.exp(cross_scores)
    cross_sums = jnp.einsum(
        "chqk,ckhd->cqhd",
        cross_weights.astype(jnp.bfloat16),
        cross_values,
        preferred_element_type=jnp.float32,
    )
    cross_totals = jnp.transpose(jnp.sum(cross_weights, axis=3), (0, 2, 1))
    cross_heads = (cross_sums / cross_totals[:, :, :, None]).reshape(tok_rows, head_count, HD)
    cross_core = (
        jnp.where(live_rows[:, None, None], cross_heads, 0.0)
        .astype(jnp.bfloat16)
        .reshape(1, tok_rows, feature_width)
    )
    return (self_core, cross_core)


def solution(mesh):
    in_specs = (
        P("dp", "ctx", "mp"),
        P("dp", "ctx", "mp"),
        P("dp", "ctx", "mp"),
        P("dp", "ctx", "mp"),
        P("dp", "ctx", None, None),
        P(("dp", "ctx"), "mp"),
        P(("dp", "ctx"), "mp"),
        P("dp", "ctx", None),
        P("dp", "ctx", None),
        P("dp"),
    )
    out_specs = (P("dp", "ctx", "mp"), P("dp", "ctx", "mp"))
    return jax.shard_map(local, mesh=mesh, in_specs=in_specs, out_specs=out_specs, check_vma=False)
```

profile of v0, /device:TPU:6, one launch (start us, length us, event | category | flops | bytes accessed | tf_op | source)
XLA Modules:
  0.0 928.9 jit_solution(18198151895259171869)
XLA Ops:
  12.1 10.4 %all-to-all-start = ((s32[16,1,1]{2,1,0:T(1,128)}), s32[16,1,1]{2,1,0:T(1,128)S(1)}, u32[]{:S(2)}, u32[]{:S(2)}) async-start(s32[16,1,1]{2,1,0:T(1,128)} %copy.76), calls=%async_computation | async-start | bytes 16384 | tf_op jit(solution)/shard_map/all_to_all | solution.py:112
  22.6 1.8 copy.69
  24.4 5.7 all-to-all-done
  31.3 1.5 bitcast_select_fusion
  33.2 0.9 gather_fusion.1
  34.3 1.2 copy-done.1
  35.6 2.8 maximum_select_fusion
  38.4 4.6 all-to-all-start.1
  43.2 0.9 copy.70
  48.9 355.5 %all-gather.13.cloned.1.call-done = bf16[128,7,1024]{2,1,0:T(8,128)(2,1)} async-done(((bf16[1,7,1024]{2,1,0:T(8,128)(2,1)}), bf16[128,7,1024]{2,1,0:T(8,128)(2,1)}) %all-gather.13.cloned.1.call-update) | async-done | bytes 1835024 | tf_op jit(solution)/shard_map/all_gather | solution.py:124
  404.4 2.7 reshape.338
  407.1 2.5 copy.77
  409.6 369.7 %all-gather.11.cloned.1.call-done = bf16[128,7,1024]{2,1,0:T(8,128)(2,1)} async-done(((bf16[1,7,1024]{2,1,0:T(8,128)(2,1)}), bf16[128,7,1024]{2,1,0:T(8,128)(2,1)}) %all-gather.11.cloned.1.call-update) | async-done | bytes 1835024 | tf_op jit(solution)/shard_map/all_gather | solution.py:125
  779.3 3.9 reshape.336
  783.2 61.9 %all-gather.7.cloned.1.call-done = bf16[1,1024,1024]{1,2,0:T(8,128)(2,1)} async-done(((bf16[1,128,1024]{1,2,0:T(8,128)(2,1)}), bf16[1,1024,1024]{1,2,0:T(8,128)(2,1)}) %all-gather.7.cloned.1.call-update) | async-done | bytes 2097168 | tf_op jit(solution)/shard_map/all_gather | solution.py:81
  845.1 58.6 %all-gather.9.cloned.1.call-done = bf16[1,1024,1024]{1,2,0:T(8,128)(2,1)} async-done(((bf16[1,128,1024]{1,2,0:T(8,128)(2,1)}), bf16[1,1024,1024]{1,2,0:T(8,128)(2,1)}) %all-gather.9.cloned.1.call-update) | async-done | bytes 2097168 | tf_op jit(solution)/shard_map/all_gather | solution.py:82
  903.7 1.2 slice-done
  905.0 2.4 conditional.2
  905.1 1.7 fusion
  907.3 3.4 conditional.3
  907.4 1.4 slice.24
  911.9 2.7 gather_fusion
  914.9 2.8 fusion.17
  919.2 1.3 multiply_reduce_fusion
  (87 shorter events, 17.0 us)
Async XLA Ops:
  7.2 23.3 %copy-start = (bf16[1,8,64,896]{3,2,1,0:T(8,128)(2,1)S(1)}, bf16[1,8,64,896]{3,2,1,0:T(8,128)(2,1)}, u32[]{:S(2)}) copy-start(bf16[1,8,64,896]{3,2,1,0:T(8,128)(2,1)} %param.20) | copy-start | bytes 2752516
  7.2 397.3 %all-gather.13.cloned.1.call-start = ((), (), s32[]{:S(2)}) async-start(), calls=%async_computation.5 | async-start | bytes 2113536 | tf_op jit(solution)/shard_map/all_gather | solution.py:124
  7.9 771.4 %all-gather.11.cloned.1.call-start = ((), (), s32[]{:S(2)}) async-start(), calls=%async_computation.4 | async-start | bytes 2113536 | tf_op jit(solution)/shard_map/all_gather | solution.py:125
  12.1 18.0 %all-to-all-start = ((s32[16,1,1]{2,1,0:T(1,128)}), s32[16,1,1]{2,1,0:T(1,128)S(1)}, u32[]{:S(2)}, u32[]{:S(2)}) async-start(s32[16,1,1]{2,1,0:T(1,128)} %copy.76), calls=%async_computation | async-start | bytes 16384 | tf_op jit(solution)/shard_map/all_to_all | solution.py:112
  22.5 822.6 %all-gather.7.cloned.1.call-start = ((), (), s32[]{:S(2)}) async-start(), calls=%async_computation.2 | async-start | bytes 2359296 | tf_op jit(solution)/shard_map/all_gather | solution.py:81
  34.1 1.5 copy-start.1
  38.4 4.7 copy-start.6
  38.4 6.2 copy-start.9
  38.4 7.7 copy-start.7
  38.4 9.1 copy-start.8
  38.4 873.5 %all-to-all-start.1 = ((bf16[16,1,128,896]{3,2,1,0:T(8,128)(2,1)}), bf16[16,1,128,896]{3,2,1,0:T(8,128)(2,1)}, u32[]{:S(2)}, u32[]{:S(2)}) async-start(bf16[16,1,128,896]{3,2,1,0:T(8,128)(2,1)} %maximum_select_fusion), calls=%async_computation.1 | async-start | bytes 7340032 | tf_op jit(solution)/shard_map/all_to_all | solution.py:119
  43.1 860.6 %all-gather.9.cloned.1.call-start = ((), (), s32[]{:S(2)}) async-start(), calls=%async_computation.3 | async-start | bytes 2359296 | tf_op jit(solution)/shard_map/all_gather | solution.py:82
  845.1 58.6 %slice-start.1 = ((bf16[1,1024,1024]{1,2,0:T(8,128)(2,1)}), bf16[1,512,1024]{1,2,0:T(8,128)(2,1)S(1)}, s32[]{:S(2)}) async-start(bf16[1,1024,1024]{1,2,0:T(8,128)(2,1)} %all-gather.7.cloned.1.call-done), calls=%async_computation.7 | async-start | bytes 2097152 | tf_op jit(solution)/shard_map/slice | solution.py:20
  903.7 1.2 slice-start
  907.3 1.9 copy-start.2
  907.3 2.0 copy-start.3
  910.7 4.0 copy-start.11
  917.7 0.6 copy-start.10
  917.7 1.5 copy-start.4
  919.2 1.3 copy-start.5
Sparse Core Ops, SparseCore 0:
  10.1 394.2 all-gather.12
  406.6 372.7 all-gather.10
  781.9 63.1 all-gather.6
  846.9 56.7 all-gather.8
where the time goes:
time: 930 us; the launch traced here: 929 us
  waiting for transfers between devices  853 us (92%)
  local copies, waits for them, and re-layouts  28.4 us (3%)
  between operations  16 us (2%)
  starting transfers between devices  15.2 us (2%)
    all_gather x1, waiting for transfers between devices, local(): lax.all_gather(value_weight, ('dp', 'ctx'), axis=0, tiled=True)  370 us
    all_gather x1, waiting for transfers between devices, local(): lax.all_gather(key_weight, ('dp', 'ctx'), axis=0, tiled=True)  356 us
    all_gather x1, waiting for transfers between devices, local(): lax.all_gather(keys, 'ctx', axis=1, tiled=True)[0]  61.9 us
    all_gather x1, waiting for transfers between devices, local(): lax.all_gather(values, 'ctx', axis=1, tiled=True)[0]  58.6 us
  transfers between devices with their start and end apart: 6, of which 5 were waited for; matrix products, arithmetic and copies ran while one was open for 3% of the time, Pallas kernels for 0%

commit v1 on v0

--- a/solution.py
+++ b/solution.py
@@ -1,3 +1,4 @@
+import functools
 import math
 import jax
 import jax.numpy as jnp
@@ -7,6 +8,15 @@
 HD = 128
 SPAN = 64
 NBR = 2
+
+
+def define_pairs_all_now(message, ax_name):
+    r2 = jnp.stack([message for _ in range(lax.axis_size(ax_name))], axis=0)
+    outcome_arr = lax.all_to_all(r2, axis_name=ax_name, split_axis=0, concat_axis=0)
+    return jnp.concatenate(outcome_arr, axis=1)
+
+
+_expand_floor = functools.partial(define_pairs_all_now, ax_name="ctx")
 
 
 def attend_block(totals, query_heads, positions, key_piece, value_piece, start):
@@ -78,7 +88,7 @@
         empty_totals(tok_rows, head_count),
         query_heads,
         positions,
-        lax.all_gather(keys, "ctx", axis=1, tiled=True)[0],
+        _expand_floor(keys)[0],
         lax.all_gather(values, "ctx", axis=1, tiled=True)[0],
         jnp.int32(0),
     )

time: 930 us -> 883 us (0.949)
  waiting for transfers between devices: 853 us -> 781 us
  blocking collectives: 0 us -> 17.8 us
    all_gather x1 -> x0, waiting for transfers between devices: 61.9 us -> none  [local(): lax.all_gather(keys, 'ctx', axis=1, tiled=True)[0]]
    all_gather x1, waiting for transfers between devices: 356 us -> 336 us  [local(): lax.all_gather(key_weight, ('dp', 'ctx'), axis=0, tiled=True)]
    all_to_all x0 -> x1, blocking collectives: none -> 17.8 us  [local(): lax.all_to_all(requests, 'dp', split_axis=0, concat_axis=0, tiled=True)]
  transfers between devices with their start and end apart: 6 -> 5, of which waited for: 5 -> 4; matrix products, arithmetic and copies ran while one was open for 3% -> 5% of each run, Pallas kernels for 0% -> 0%
where the time goes in v1:
time: 883 us; the launch traced here: 882 us
  waiting for transfers between devices  781 us (88%)
  local copies, waits for them, and re-layouts  36 us (4%)
  blocking collectives  17.8 us (2%)
  between operations  15.9 us (2%)
  other arithmetic  12.4 us (1%)
  starting transfers between devices  10.4 us (1%)
    all_gather x1, waiting for transfers between devices, local(): lax.all_gather(value_weight, ('dp', 'ctx'), axis=0, tiled=True)  372 us
    all_gather x1, waiting for transfers between devices, local(): lax.all_gather(key_weight, ('dp', 'ctx'), axis=0, tiled=True)  336 us
    all_gather x1, waiting for transfers between devices, local(): lax.all_gather(values, 'ctx', axis=1, tiled=True)[0]  60.5 us
    all_to_all x1, blocking collectives, local(): lax.all_to_all(requests, 'dp', split_axis=0, concat_axis=0, tiled=True)  17.8 us
  transfers between devices with their start and end apart: 5, of which 4 were waited for; matrix products, arithmetic and copies ran while one was open for 5% of the time, Pallas kernels for 0%

profile of v1, /device:TPU:6, one launch (start us, length us, event | category | flops | bytes accessed | tf_op | source)
XLA Modules:
  0.0 882.2 jit_solution(17974770619590664866)
XLA Ops:
  11.3 17.8 %all_to_all.16 = s32[16,1,1]{2,1,0:T(1,128)S(1)} all-to-all(s32[16,1,1]{2,1,0:T(1,128)S(1)} %copy.75), channel_id=1, replica_groups=mesh['dp'=16,'ctx'=8,'mp'=4] {'dp'}, dimensions={0} | all-to-all | bytes 128 | tf_op jit(solution)/shard_map/all_to_all | solution.py:122
  29.1 2.6 stack.2
  31.6 5.8 all-to-all-start
  38.6 2.0 gather_fusion.2
  40.6 3.0 bitcast_select_fusion
  44.0 2.0 gather_fusion.1
  46.0 1.9 bitcast_select_fusion.1
  48.1 2.8 maximum_select_fusion
  50.9 12.0 %all-to-all-done = bf16[8,1,128,1024]{3,2,1,0:T(8,128)(2,1)S(1)} async-done(((bf16[8,1,128,1024]{3,2,1,0:T(8,128)(2,1)}), bf16[8,1,128,1024]{3,2,1,0:T(8,128)(2,1)S(1)}, u32[]{:S(2)}, u32[]{:S(2)}) %all-to-all-start) | async-done | bytes 2097184 | tf_op jit(solution)/shard_map/all_to_all | solution.py:15
  62.9 4.5 all-to-all-start.2
  71.9 1.7 copy.89
  75.5 335.5 %all-gather.10.cloned.1.call-done = bf16[128,7,1024]{2,1,0:T(8,128)(2,1)} async-done(((bf16[1,7,1024]{2,1,0:T(8,128)(2,1)}), bf16[128,7,1024]{2,1,0:T(8,128)(2,1)}) %all-gather.10.cloned.1.call-update) | async-done | bytes 1835024 | tf_op jit(solution)/shard_map/all_gather | solution.py:134
  411.1 3.9 reshape.341
  414.9 3.9 copy.76
  418.8 371.5 %all-gather.8.cloned.1.call-done = bf16[128,7,1024]{2,1,0:T(8,128)(2,1)} async-done(((bf16[1,7,1024]{2,1,0:T(8,128)(2,1)}), bf16[128,7,1024]{2,1,0:T(8,128)(2,1)}) %all-gather.8.cloned.1.call-update) | async-done | bytes 1835024 | tf_op jit(solution)/shard_map/all_gather | solution.py:135
  790.3 3.9 reshape.339
  795.5 60.5 %all-gather.6.cloned.1.call-done = bf16[1,1024,1024]{1,2,0:T(8,128)(2,1)} async-done(((bf16[1,128,1024]{1,2,0:T(8,128)(2,1)}), bf16[1,1024,1024]{1,2,0:T(8,128)(2,1)}) %all-gather.6.cloned.1.call-update) | async-done | bytes 2097168 | tf_op jit(solution)/shard_map/all_gather | solution.py:92
  857.6 2.4 conditional.2
  857.7 1.8 fusion
  860.0 3.9 conditional.3
  860.0 1.3 slice.24
  865.2 2.7 gather_fusion
  868.2 2.8 fusion.21
  872.5 1.3 multiply_reduce_fusion
  (86 shorter events, 20.8 us)
Async XLA Ops:
  7.2 31.4 %copy-start = (bf16[1,8,64,896]{3,2,1,0:T(8,128)(2,1)S(1)}, bf16[1,8,64,896]{3,2,1,0:T(8,128)(2,1)}, u32[]{:S(2)}) copy-start(bf16[1,8,64,896]{3,2,1,0:T(8,128)(2,1)} %param.20) | copy-start | bytes 2752516
  7.2 403.9 %all-gather.10.cloned.1.call-start = ((), (), s32[]{:S(2)}) async-start(), calls=%async_computation.5 | async-start | bytes 2113536 | tf_op jit(solution)/shard_map/all_gather | solution.py:134
  10.5 58.5 %copy-start.9 = (s32[4]{0:T(128)}, s32[4]{0:T(128)S(1)}, u32[]{:S(2)}) copy-start(s32[4]{0:T(128)S(1)} %convert_reduce_fusion) | copy-start | bytes 52
  31.6 31.3 %all-to-all-start = ((bf16[8,1,128,1024]{3,2,1,0:T(8,128)(2,1)}), bf16[8,1,128,1024]{3,2,1,0:T(8,128)(2,1)S(1)}, u32[]{:S(2)}, u32[]{:S(2)}) async-start(bf16[8,1,128,1024]{3,2,1,0:T(8,128)(2,1)} %stack.2), calls=%async_computation | async-start | bytes 4194304 | tf_op jit(solution)/shard_map/all_to_all | solution.py:15
  37.4 752.9 %all-gather.8.cloned.1.call-start = ((), (), s32[]{:S(2)}) async-start(), calls=%async_computation.4 | async-start | bytes 2113536 | tf_op jit(solution)/shard_map/all_gather | solution.py:135
  46.0 2.1 copy-start.1
  50.9 16.6 %copy-start.5 = (bf16[1,128,1024]{2,1,0:T(8,128)(2,1)S(1)}, bf16[1,128,1024]{2,1,0:T(8,128)(2,1)}, u32[]{:S(2)}) copy-start(bf16[1,128,1024]{2,1,0:T(8,128)(2,1)} %param.18) | copy-start | bytes 786436
  50.9 18.0 %copy-start.8 = (s32[1,2,2]{2,1,0:T(2,128)S(1)}, s32[1,2,2]{2,1,0:T(2,128)}, u32[]{:S(2)}) copy-start(s32[1,2,2]{2,1,0:T(2,128)} %param.23) | copy-start | bytes 52
  50.9 19.5 %copy-start.6 = (bf16[1,128,1024]{2,1,0:T(8,128)(2,1)S(1)}, bf16[1,128,1024]{2,1,0:T(8,128)(2,1)}, u32[]{:S(2)}) copy-start(bf16[1,128,1024]{2,1,0:T(8,128)(2,1)} %param.16) | copy-start | bytes 786436
  62.9 802.3 %all-to-all-start.2 = ((bf16[16,1,128,896]{3,2,1,0:T(8,128)(2,1)}), bf16[16,1,128,896]{3,2,1,0:T(8,128)(2,1)}, u32[]{:S(2)}, u32[]{:S(2)}) async-start(bf16[16,1,128,896]{3,2,1,0:T(8,128)(2,1)} %maximum_select_fusion), calls=%async_computation.2 | async-start | bytes 7340032 | tf_op jit(solution)/shard_map/all_to_all | solution.py:129
  67.4 788.6 %all-gather.6.cloned.1.call-start = ((), (), s32[]{:S(2)}) async-start(), calls=%async_computation.3 | async-start | bytes 2359296 | tf_op jit(solution)/shard_map/all_gather | solution.py:92
  856.0 1.2 slice-start
  856.0 1.5 copy-start.3
  861.4 1.0 copy-start.7
  863.9 4.0 copy-start.11
  871.0 0.6 copy-start.10
  871.0 1.5 copy-start.2
  872.5 1.3 copy-start.4
Sparse Core Ops, SparseCore 0:
  10.1 400.9 all-gather.9
  413.2 377.0 all-gather.7
  792.9 63.1 all-gather.5
